TPU v7x, 768 devices: a whole 4x8x12 slice. The times are simulated.
768 devices in a mesh: depth: 64 (over x, y, core), rows: 12 (over z).
Axes of the slice: x: 4, y: 8, z: 12, core: 2. Of those that a mesh axis runs over, the one named last changes fastest.
Arguments:
- density: float32 [512, 96, 1024], P('depth', 'rows'), may hold values from -6 to 6
- material: int32 [512, 96, 1024], P('depth', 'rows'), may hold values from 0 to 15
- absorption: float32 [16], replicated, may hold values from 0.5 to 4
- emission: float32 [8, 16], replicated, may hold values from 1 to 8
- shard_rank: int32 [64], replicated, may hold values from 0 to 63, each once
Outputs:
- smoothed: float32 [512, 96, 1024], P('depth', 'rows')
- band_image: float32 [8, 96, 1024], P(None, 'rows', 'depth')
- transmittance: float32 [96, 1024], P('rows', 'depth')
Inputs may be any that keep to these rules, and one draw needn't show every extreme that they name: `shard_rank`: each value names one depth slab's rank, every rank once.
All inputs are finite; a program needn't handle non-finite values.
Results may differ from a plain program's by a relative error of at most 0.0003.
Values sent between devices are 32-bit elements; how exact they have to be, the bound alone decides.
A program may use at most 32 MiB of HBM per device.

v0:
```python
import jax
import jax.numpy as jnp
from jax import lax
from jax.sharding import PartitionSpec as P

SWEEPS = 4


time_step = 0.16
edge_scale = 1.5
light_z = 0.6
light_y = 0.48
light_x = 0.64
step_scale = 1.2


def with_halo(block, sides, width):
    for axis, dim in sides:
        count = lax.axis_size(axis)
        forward = [(i, i + 1) for i in range(count - 1)]
        backward = [(target, source) for source, target in forward]
        low = lax.ppermute(
            lax.slice_in_dim(block, block.shape[dim] - width, None, axis=dim), axis, forward
        )
        high = lax.ppermute(lax.slice_in_dim(block, 0, width, axis=dim), axis, backward)
        block = jnp.concatenate([low, block, high], axis=dim)
    return block


def conduct(diff):
    return diff / (1.0 + diff * diff * (1.0 / (edge_scale * edge_scale)))


def diffuse(padded):
    centre = padded[1:-1, 1:-1, 1:-1]
    total = conduct(padded[2:, 1:-1, 1:-1] - centre) + conduct(padded[:-2, 1:-1, 1:-1] - centre)
    total = (
        total + conduct(padded[1:-1, 2:, 1:-1] - centre) + conduct(padded[1:-1, :-2, 1:-1] - centre)
    )
    total = (
        total + conduct(padded[1:-1, 1:-1, 2:] - centre) + conduct(padded[1:-1, 1:-1, :-2] - centre)
    )
    return centre + time_step * total


def shading_of(padded):
    grad_z = (padded[2:, 1:-1, 1:-1] - padded[:-2, 1:-1, 1:-1]) * 0.5
    grad_y = (padded[1:-1, 2:, 1:-1] - padded[1:-1, :-2, 1:-1]) * 0.5
    grad_x = (padded[1:-1, 1:-1, 2:] - padded[1:-1, 1:-1, :-2]) * 0.5
    lambert = (grad_z * light_z + grad_y * light_y + grad_x * light_x) / jnp.sqrt(
        grad_z * grad_z + grad_y * grad_y + grad_x * grad_x + 1.0
    )
    return 0.55 + 0.45 * lambert


def pad_columns(field):
    return jnp.pad(field, ((0, 0), (0, 0), (1, 1)))


def with_faces(field):
    extended = with_halo(field, (("depth", 0), ("rows", 1)), 1)
    return pad_columns(extended)


def body(density, material, absorption, emission, shard_rank):
    slab_cells, row_count, columns = density.shape
    shard_count = lax.axis_size("depth")
    depth_index = lax.axis_index("depth")
    nz_total = slab_cells * shard_count
    field = density
    for sweep_index in range(SWEEPS):
        field = diffuse(with_faces(field))
    shading = shading_of(with_faces(field))
    step_len = step_scale / nz_total
    table = jnp.concatenate([absorption[None, :], emission], axis=0)
    class_ids = jnp.arange(table.shape[1], dtype=jnp.int32)

    def march(state, layer):
        depth_sum, radiance = state
        layer_field, layer_shading, layer_material = layer
        one_hot = (layer_material[None, :, :] == class_ids[:, None, None]).astype(jnp.float32)
        lookup = jnp.einsum("bk,kyx->byx", table, one_hot, precision=lax.Precision.HIGHEST)
        optical = lookup[0] * jax.nn.softplus(layer_field) * step_len
        opacity = 1.0 - jnp.exp(-optical)
        contrib = jnp.exp(-depth_sum) * opacity * layer_shading
        radiance = radiance + contrib[None] * lookup[1:]
        return ((depth_sum + optical, radiance), None)

    start_state = (
        jnp.zeros((row_count, columns), jnp.float32),
        jnp.zeros((emission.shape[0], row_count, columns), jnp.float32),
    )
    (slab_depth, slab_colour), unused = lax.scan(march, start_state, (field, shading, material))
    own_columns = columns // shard_count
    my_rank = jnp.sum(
        jnp.where(jnp.arange(shard_count, dtype=jnp.int32) == depth_index, shard_rank, 0)
    )
    block_rows = lax.all_gather(slab_depth[None], "depth", axis=0, tiled=True)
    ahead = (shard_rank < my_rank).astype(jnp.float32)
    prior = jnp.sum(ahead[:, None, None] * block_rows, axis=0)
    overall = jnp.sum(block_rows, axis=0)
    prior, overall = (prior, overall)
    weighted = slab_colour * jnp.exp(-prior)[None]
    band_image = lax.psum_scatter(weighted, "depth", scatter_dimension=2, tiled=True)
    transmittance = lax.dynamic_slice_in_dim(
        jnp.exp(-overall), depth_index * own_columns, own_columns, 1
    )
    return (field, band_image, transmittance)


def solution(mesh):
    in_specs = (P("depth", "rows", None), P("depth", "rows", None), P(), P(), P())
    out_specs = (P("depth", "rows", None), P(None, "rows", "depth"), P("rows", "depth"))
    return jax.shard_map(body, mesh=mesh, in_specs=in_specs, out_specs=out_specs, check_vma=False)
```

profile of v0, /device:TPU:1, one launch (start us, length us, event | category | flops | bytes accessed | tf_op | source)
XLA Modules:
  0.0 376.9 jit_solution(401754014105586801)
XLA Ops:
  7.2 0.8 fusion.38
  8.0 4.6 %collective-permute-start.1 = (f32[1,8,1024]{2,1,0:T(8,128)S(1)}, f32[1,8,1024]{2,1,0:T(8,128)S(1)}, u32[]{:S(2)}, u32[]{:S(2)}) collective-permute-start(f32[1,8,1024]{2,1,0:T(8,128)S(1)} %get-tuple-element.111), channel_id=1, source_target_pairs={{0,12},{12,24},{24,36},{36,48},{48,60},{60,72},{72,84},{84,96},{96... | collective-permute-start | bytes 98312 | tf_op jit(solution)/shard_map/ppermute | solution.py:22
  12.6 9.1 %collective-permute-start = (f32[1,8,1024]{2,1,0:T(8,128)S(1)}, f32[1,8,1024]{2,1,0:T(8,128)S(1)}, u32[]{:S(2)}, u32[]{:S(2)}) collective-permute-start(f32[1,8,1024]{2,1,0:T(8,128)S(1)} %get-tuple-element.110), channel_id=1, source_target_pairs={{12,0},{24,12},{36,24},{48,36},{60,48},{72,60},{84,72},{96,84},{10... | collective-permute-start | bytes 98312 | tf_op jit(solution)/shard_map/ppermute | solution.py:25
  21.7 1.0 constant_dynamic-update-slice_fusion.1
  22.8 1.3 collective-permute-start.3
  24.1 1.3 collective-permute-start.2
  25.4 3.4 collective-permute-done.2
  29.8 1.9 collective-permute-start.5
  31.8 2.6 collective-permute-start.4
  34.4 2.6 collective-permute-done.4
  37.1 3.6 collective-permute-start.7
  40.7 1.3 collective-permute-start.6
  42.0 5.3 %collective-permute-done.6 = f32[10,1,1024]{2,1,0:T(1,128)S(1)} collective-permute-done((f32[10,1,1024]{2,1,0:T(1,128)S(1)}, f32[10,1,1024]{2,1,0:T(1,128)S(1)}, u32[]{:S(2)}, u32[]{:S(2)}) %collective-permute-start.6) | collective-permute-done | bytes 40992 | tf_op jit(solution)/shard_map/ppermute | solution.py:25
  48.2 3.1 collective-permute-start.9
  51.3 1.9 collective-permute-start.8
  53.3 3.3 collective-permute-done.8
  56.6 4.9 %collective-permute-start.11 = (f32[10,1,1024]{2,1,0:T(1,128)S(1)}, f32[10,1,1024]{2,1,0:T(1,128)S(1)}, u32[]{:S(2)}, u32[]{:S(2)}) collective-permute-start(f32[10,1,1024]{2,1,0:T(1,128)S(1)} %get-tuple-element.96), channel_id=1, source_target_pairs={{0,1},{1,2},{2,3},{3,4},{4,5},{5,6},{6,7},{7,8},{8,9},{9,10},{10,1... | collective-permute-start | bytes 122888 | tf_op jit(solution)/shard_map/ppermute | solution.py:22
  61.5 1.3 collective-permute-start.10
  62.8 3.7 collective-permute-done.10
  67.5 3.1 collective-permute-start.13
  70.6 1.9 collective-permute-start.12
  72.5 3.3 collective-permute-done.12
  75.9 4.4 %collective-permute-start.15 = (f32[10,1,1024]{2,1,0:T(1,128)S(1)}, f32[10,1,1024]{2,1,0:T(1,128)S(1)}, u32[]{:S(2)}, u32[]{:S(2)}) collective-permute-start(f32[10,1,1024]{2,1,0:T(1,128)S(1)} %get-tuple-element.94), channel_id=1, source_target_pairs={{0,1},{1,2},{2,3},{3,4},{4,5},{5,6},{6,7},{7,8},{8,9},{9,10},{10,1... | collective-permute-start | bytes 122888 | tf_op jit(solution)/shard_map/ppermute | solution.py:22
  80.2 1.3 collective-permute-start.14
  81.5 3.7 collective-permute-done.14
  86.2 3.1 collective-permute-start.17
  89.3 1.9 collective-permute-start.16
  91.2 3.3 collective-permute-done.16
  94.6 3.7 collective-permute-start.19
  98.3 1.3 collective-permute-start.18
  99.7 3.7 collective-permute-done.18
  104.1 11.0 %while.13 = (s32[]{:T(128)}, f32[8,1024]{1,0:T(8,128)S(1)}, f32[8,8,1024]{2,0,1:T(8,128)S(1)}, s32[8,8,1024]{2,1,0:T(8,128)}, f32[9,16]{1,0:T(8,128)S(1)}, /*ind...) while((s32[]{:T(128)}, f32[8,1024]{1,0:T(8,128)S(1)}, ...), condition=%wide.region_1.2_spmd.clone, body=%wide.region_0.1_spmd.clone.sunk | while | flops 14606339 | bytes 1475256 | solution.py:93
  104.2 0.8 dynamic-slice_bitcast_fusion.2
  105.5 0.8 dynamic-slice_bitcast_fusion.2
  106.9 0.8 dynamic-slice_bitcast_fusion.2
  108.3 0.8 dynamic-slice_bitcast_fusion.2
  109.6 0.8 dynamic-slice_bitcast_fusion.2
  111.0 0.8 dynamic-slice_bitcast_fusion.2
  112.4 0.8 dynamic-slice_bitcast_fusion.2
  113.7 0.8 dynamic-slice_bitcast_fusion.2
  117.1 94.2 %all-gather.3.cloned.1.call-done = f32[512,1024]{1,0:T(8,128)} async-done(((f32[8,1024]{1,0:T(8,128)}), f32[512,1024]{1,0:T(8,128)}) %all-gather.3.cloned.1.call-update) | async-done | bytes 2097168 | tf_op jit(solution)/shard_map/all_gather | solution.py:98
  211.3 1.8 bitcast_reduce_fusion
  213.4 2.6 copy.10
  216.0 3.9 %reshape.15 = f32[1024,64]{1,0:T(8,128)} reshape(f32[1024,8,8]{2,1,0:T(8,128)} %bitcast.55) | data formatting | bytes 524288
  219.9 0.7 fusion.31
  220.6 148.0 %reduce-scatter.4.cloned.1.call-done = f32[16,64]{1,0:T(8,128)} async-done(((f32[1024,64]{1,0:T(8,128)}), f32[16,64]{1,0:T(8,128)}) %reduce-scatter.4.cloned.1.call-update) | async-done | bytes 4112
  368.6 0.8 reshape.16
  369.4 0.7 copy.11
  (87 shorter events, 11.7 us)
Async XLA Ops:
  7.2 22.1 %copy-start.1 = (f32[8,8,1024]{2,1,0:T(8,128)S(1)}, f32[8,8,1024]{2,1,0:T(8,128)}, u32[]{:S(2)}) copy-start(f32[8,8,1024]{2,1,0:T(8,128)} %param.7) | copy-start | bytes 786436
  7.2 204.2 %all-gather.3.cloned.1.call-start = ((), (), s32[]{:S(2)}) async-start(), calls=%async_computation.1 | async-start | bytes 2129920 | tf_op jit(solution)/shard_map/all_gather | solution.py:98
  8.0 13.7 %collective-permute-start.1 = (f32[1,8,1024]{2,1,0:T(8,128)S(1)}, f32[1,8,1024]{2,1,0:T(8,128)S(1)}, u32[]{:S(2)}, u32[]{:S(2)}) collective-permute-start(f32[1,8,1024]{2,1,0:T(8,128)S(1)} %get-tuple-element.111), channel_id=1, source_target_pairs={{0,12},{12,24},{24,36},{36,48},{48,60},{60,72},{72,84},{84,96},{96... | collective-permute-start | bytes 98312 | tf_op jit(solution)/shard_map/ppermute | solution.py:22
  12.6 10.1 %collective-permute-start = (f32[1,8,1024]{2,1,0:T(8,128)S(1)}, f32[1,8,1024]{2,1,0:T(8,128)S(1)}, u32[]{:S(2)}, u32[]{:S(2)}) collective-permute-start(f32[1,8,1024]{2,1,0:T(8,128)S(1)} %get-tuple-element.110), channel_id=1, source_target_pairs={{12,0},{24,12},{36,24},{48,36},{60,48},{72,60},{84,72},{96,84},{10... | collective-permute-start | bytes 98312 | tf_op jit(solution)/shard_map/ppermute | solution.py:25
  22.8 2.6 collective-permute-start.3
  24.1 4.7 %collective-permute-start.2 = (f32[10,1,1024]{2,1,0:T(1,128)S(1)}, f32[10,1,1024]{2,1,0:T(1,128)S(1)}, u32[]{:S(2)}, u32[]{:S(2)}) collective-permute-start(f32[10,1,1024]{2,1,0:T(1,128)S(1)} %get-tuple-element.101), channel_id=1, source_target_pairs={{1,0},{2,1},{3,2},{4,3},{5,4},{6,5},{7,6},{8,7},{9,8},{10,9},{11,1... | collective-permute-start | bytes 122888 | tf_op jit(solution)/shard_map/ppermute | solution.py:25
  29.8 4.5 %collective-permute-start.5 = (f32[1,8,1024]{2,1,0:T(8,128)S(1)}, f32[1,8,1024]{2,1,0:T(8,128)S(1)}, u32[]{:S(2)}, u32[]{:S(2)}) collective-permute-start(f32[1,8,1024]{2,1,0:T(8,128)S(1)} %get-tuple-element.108), channel_id=1, source_target_pairs={{0,12},{12,24},{24,36},{36,48},{48,60},{60,72},{72,84},{84,96},{96... | collective-permute-start | bytes 98312 | tf_op jit(solution)/shard_map/ppermute | solution.py:22
  31.8 5.2 %collective-permute-start.4 = (f32[1,8,1024]{2,1,0:T(8,128)S(1)}, f32[1,8,1024]{2,1,0:T(8,128)S(1)}, u32[]{:S(2)}, u32[]{:S(2)}) collective-permute-start(f32[1,8,1024]{2,1,0:T(8,128)S(1)} %get-tuple-element.109), channel_id=1, source_target_pairs={{12,0},{24,12},{36,24},{48,36},{60,48},{72,60},{84,72},{96,84},{10... | collective-permute-start | bytes 98312 | tf_op jit(solution)/shard_map/ppermute | solution.py:25
  37.1 4.9 %collective-permute-start.7 = (f32[10,1,1024]{2,1,0:T(1,128)S(1)}, f32[10,1,1024]{2,1,0:T(1,128)S(1)}, u32[]{:S(2)}, u32[]{:S(2)}) collective-permute-start(f32[10,1,1024]{2,1,0:T(1,128)S(1)} %get-tuple-element.98), channel_id=1, source_target_pairs={{0,1},{1,2},{2,3},{3,4},{4,5},{5,6},{6,7},{7,8},{8,9},{9,10},{10,1... | collective-permute-start | bytes 122888 | tf_op jit(solution)/shard_map/ppermute | solution.py:22
  40.7 6.6 %collective-permute-start.6 = (f32[10,1,1024]{2,1,0:T(1,128)S(1)}, f32[10,1,1024]{2,1,0:T(1,128)S(1)}, u32[]{:S(2)}, u32[]{:S(2)}) collective-permute-start(f32[10,1,1024]{2,1,0:T(1,128)S(1)} %get-tuple-element.99), channel_id=1, source_target_pairs={{1,0},{2,1},{3,2},{4,3},{5,4},{6,5},{7,6},{8,7},{9,8},{10,9},{11,1... | collective-permute-start | bytes 122888 | tf_op jit(solution)/shard_map/ppermute | solution.py:25
  48.2 5.0 %collective-permute-start.9 = (f32[1,8,1024]{2,1,0:T(8,128)S(1)}, f32[1,8,1024]{2,1,0:T(8,128)S(1)}, u32[]{:S(2)}, u32[]{:S(2)}) collective-permute-start(f32[1,8,1024]{2,1,0:T(8,128)S(1)} %get-tuple-element.106), channel_id=1, source_target_pairs={{0,12},{12,24},{24,36},{36,48},{48,60},{60,72},{72,84},{84,96},{96... | collective-permute-start | bytes 98312 | tf_op jit(solution)/shard_map/ppermute | solution.py:22
  51.3 5.2 %collective-permute-start.8 = (f32[1,8,1024]{2,1,0:T(8,128)S(1)}, f32[1,8,1024]{2,1,0:T(8,128)S(1)}, u32[]{:S(2)}, u32[]{:S(2)}) collective-permute-start(f32[1,8,1024]{2,1,0:T(8,128)S(1)} %get-tuple-element.107), channel_id=1, source_target_pairs={{12,0},{24,12},{36,24},{48,36},{60,48},{72,60},{84,72},{96,84},{10... | collective-permute-start | bytes 98312 | tf_op jit(solution)/shard_map/ppermute | solution.py:25
  56.6 6.2 %collective-permute-start.11 = (f32[10,1,1024]{2,1,0:T(1,128)S(1)}, f32[10,1,1024]{2,1,0:T(1,128)S(1)}, u32[]{:S(2)}, u32[]{:S(2)}) collective-permute-start(f32[10,1,1024]{2,1,0:T(1,128)S(1)} %get-tuple-element.96), channel_id=1, source_target_pairs={{0,1},{1,2},{2,3},{3,4},{4,5},{5,6},{6,7},{7,8},{8,9},{9,10},{10,1... | collective-permute-start | bytes 122888 | tf_op jit(solution)/shard_map/ppermute | solution.py:22
  61.5 5.0 %collective-permute-start.10 = (f32[10,1,1024]{2,1,0:T(1,128)S(1)}, f32[10,1,1024]{2,1,0:T(1,128)S(1)}, u32[]{:S(2)}, u32[]{:S(2)}) collective-permute-start(f32[10,1,1024]{2,1,0:T(1,128)S(1)} %get-tuple-element.97), channel_id=1, source_target_pairs={{1,0},{2,1},{3,2},{4,3},{5,4},{6,5},{7,6},{8,7},{9,8},{10,9},{11,1... | collective-permute-start | bytes 122888 | tf_op jit(solution)/shard_map/ppermute | solution.py:25
  67.0 32.7 %copy-start.3 = (f32[8,16]{1,0:T(8,128)S(1)}, f32[8,16]{1,0:T(8,128)}, u32[]{:S(2)}) copy-start(f32[8,16]{1,0:T(8,128)} %param.10) | copy-start | bytes 1540
  67.0 32.7 %copy-start.4 = (f32[16]{0:T(128)S(1)}, f32[16]{0:T(128)}, u32[]{:S(2)}) copy-start(f32[16]{0:T(128)} %param.9) | copy-start | bytes 196
  67.5 5.0 %collective-permute-start.13 = (f32[1,8,1024]{2,1,0:T(8,128)S(1)}, f32[1,8,1024]{2,1,0:T(8,128)S(1)}, u32[]{:S(2)}, u32[]{:S(2)}) collective-permute-start(f32[1,8,1024]{2,1,0:T(8,128)S(1)} %get-tuple-element.104), channel_id=1, source_target_pairs={{0,12},{12,24},{24,36},{36,48},{48,60},{60,72},{72,84},{84,96},{96... | collective-permute-start | bytes 98312 | tf_op jit(solution)/shard_map/ppermute | solution.py:22
  70.6 5.2 %collective-permute-start.12 = (f32[1,8,1024]{2,1,0:T(8,128)S(1)}, f32[1,8,1024]{2,1,0:T(8,128)S(1)}, u32[]{:S(2)}, u32[]{:S(2)}) collective-permute-start(f32[1,8,1024]{2,1,0:T(8,128)S(1)} %get-tuple-element.105), channel_id=1, source_target_pairs={{12,0},{24,12},{36,24},{48,36},{60,48},{72,60},{84,72},{96,84},{10... | collective-permute-start | bytes 98312 | tf_op jit(solution)/shard_map/ppermute | solution.py:25
  75.9 5.7 %collective-permute-start.15 = (f32[10,1,1024]{2,1,0:T(1,128)S(1)}, f32[10,1,1024]{2,1,0:T(1,128)S(1)}, u32[]{:S(2)}, u32[]{:S(2)}) collective-permute-start(f32[10,1,1024]{2,1,0:T(1,128)S(1)} %get-tuple-element.94), channel_id=1, source_target_pairs={{0,1},{1,2},{2,3},{3,4},{4,5},{5,6},{6,7},{7,8},{8,9},{9,10},{10,1... | collective-permute-start | bytes 122888 | tf_op jit(solution)/shard_map/ppermute | solution.py:22
  80.2 5.0 %collective-permute-start.14 = (f32[10,1,1024]{2,1,0:T(1,128)S(1)}, f32[10,1,1024]{2,1,0:T(1,128)S(1)}, u32[]{:S(2)}, u32[]{:S(2)}) collective-permute-start(f32[10,1,1024]{2,1,0:T(1,128)S(1)} %get-tuple-element.95), channel_id=1, source_target_pairs={{1,0},{2,1},{3,2},{4,3},{5,4},{6,5},{7,6},{8,7},{9,8},{10,9},{11,1... | collective-permute-start | bytes 122888 | tf_op jit(solution)/shard_map/ppermute | solution.py:25
  86.2 5.0 %collective-permute-start.17 = (f32[1,8,1024]{2,1,0:T(8,128)S(1)}, f32[1,8,1024]{2,1,0:T(8,128)S(1)}, u32[]{:S(2)}, u32[]{:S(2)}) collective-permute-start(f32[1,8,1024]{2,1,0:T(8,128)S(1)} %get-tuple-element.102), channel_id=1, source_target_pairs={{0,12},{12,24},{24,36},{36,48},{48,60},{60,72},{72,84},{84,96},{96... | collective-permute-start | bytes 98312 | tf_op jit(solution)/shard_map/ppermute | solution.py:22
  89.3 5.2 %collective-permute-start.16 = (f32[1,8,1024]{2,1,0:T(8,128)S(1)}, f32[1,8,1024]{2,1,0:T(8,128)S(1)}, u32[]{:S(2)}, u32[]{:S(2)}) collective-permute-start(f32[1,8,1024]{2,1,0:T(8,128)S(1)} %get-tuple-element.103), channel_id=1, source_target_pairs={{12,0},{24,12},{36,24},{48,36},{60,48},{72,60},{84,72},{96,84},{10... | collective-permute-start | bytes 98312 | tf_op jit(solution)/shard_map/ppermute | solution.py:25
  94.6 5.1 %collective-permute-start.19 = (f32[10,1,1024]{2,1,0:T(1,128)S(1)}, f32[10,1,1024]{2,1,0:T(1,128)S(1)}, u32[]{:S(2)}, u32[]{:S(2)}) collective-permute-start(f32[10,1,1024]{2,1,0:T(1,128)S(1)} %get-tuple-element.92), channel_id=1, source_target_pairs={{0,1},{1,2},{2,3},{3,4},{4,5},{5,6},{6,7},{7,8},{8,9},{9,10},{10,1... | collective-permute-start | bytes 122888 | tf_op jit(solution)/shard_map/ppermute | solution.py:22
  98.3 5.0 %collective-permute-start.18 = (f32[10,1,1024]{2,1,0:T(1,128)S(1)}, f32[10,1,1024]{2,1,0:T(1,128)S(1)}, u32[]{:S(2)}, u32[]{:S(2)}) collective-permute-start(f32[10,1,1024]{2,1,0:T(1,128)S(1)} %get-tuple-element.93), channel_id=1, source_target_pairs={{1,0},{2,1},{3,2},{4,3},{5,4},{6,5},{7,6},{8,7},{9,8},{10,9},{11,1... | collective-permute-start | bytes 122888 | tf_op jit(solution)/shard_map/ppermute | solution.py:25
  104.1 11.7 %copy-start.5 = (s32[64]{0:T(128)S(1)}, s32[64]{0:T(128)}, u32[]{:S(2)}) copy-start(s32[64]{0:T(128)} %param.11) | copy-start | bytes 772
  115.1 0.6 copy-start.2
  115.1 100.9 %copy-start = (f32[8,8,1024]{2,1,0:T(8,128)}, f32[8,8,1024]{2,1,0:T(8,128)S(1)}, u32[]{:S(2)}) copy-start(f32[8,8,1024]{2,1,0:T(8,128)S(1)} %get-tuple-element.188) | copy-start | bytes 786436
  115.7 252.8 %reduce-scatter.4.cloned.1.call-start = ((), (), s32[]{:S(2)}) async-start(), calls=%async_computation.2 | async-start | bytes 532480
Sparse Core Ops, SparseCore 0:
  115.9 95.4 all-gather.2
  220.1 148.4 reduce-scatter.3
where the time goes:
time: 382 us; the launch traced here: 377 us
  waiting for transfers between devices  275 us (72%)
  starting transfers between devices  57.5 us (15%)
  local copies, waits for them, and re-layouts  16.8 us (4%)
  between operations  14.6 us (4%)
  other arithmetic  10.3 us (3%)
    unnamed x3, waiting for transfers between devices  148 us
    all_gather x1, waiting for transfers between devices, body(): block_rows = lax.all_gather(slab_depth[None], 'depth', axis=0, tiled=True)  94.2 us
    ppermute x10, starting transfers between devices, with_halo(): lax.ppermute(lax.slice_in_dim(block, block.shape[dim] - width, None, axis...  33.5 us
    ppermute x10, waiting for transfers between devices, with_halo(): lax.ppermute(lax.slice_in_dim(block, 0, width, axis=dim), axis, backward)  32.3 us
    ppermute x10, starting transfers between devices, with_halo(): lax.ppermute(lax.slice_in_dim(block, 0, width, axis=dim), axis, backward)  23.9 us
    unnamed x18, local copies, waits for them, and re-layouts  9.63 us
  transfers between devices with their start and end apart: 22, of which 11 were waited for; matrix products, arithmetic and copies ran while one was open for 1% of the time, Pallas kernels for 0%

commit v1 on v0

v1 whole, which is shorter than its diff:
```python
import functools

import jax
import jax.numpy as jnp
from jax import lax
from jax.experimental import pallas as pl
from jax.experimental.pallas import tpu as pltpu
from jax.sharding import PartitionSpec as P

MESH = pl.DeviceIdType.MESH
SWEEPS = 4
LANES = 128
SUB = 8

time_step = 0.16
edge_scale = 1.5
light_z = 0.6
light_y = 0.48
light_x = 0.64
step_scale = 1.2


def conduct(diff):
    return diff / (1.0 + diff * diff * (1.0 / (edge_scale * edge_scale)))


def roll(value, shift, axis):
    return pltpu.roll(value, shift % value.shape[axis], axis)


def gather(table, index):
    return jnp.take_along_axis(table, index, axis=1, mode="promise_in_bounds")


def kernel(
    n, n_rows, x_size,
    density, material, absorption, emission, rank,
    smoothed_out, band_out, trans_out,
    a0, a1, b0, b1, flux_a, flux_b, mat, face_z, face_y, pack_y, weight, tables, swap,
    colour_send, depth_send, colour_recv, depth_recv, slab_weight,
    local_sem, halo_send, halo_recv, face_send, face_recv, a2a_send, a2a_recv,
):
    slab, bands = SUB, emission.shape[0]
    tiles = x_size // LANES
    own = x_size // n
    group = LANES // own
    d = lax.axis_index("depth")
    r = lax.axis_index("rows")
    d_up, d_down = lax.rem(d + 1, n), lax.rem(d + n - 1, n)
    r_up, r_down = lax.rem(r + 1, n_rows), lax.rem(r + n_rows - 1, n_rows)

    local = [
        pltpu.make_async_copy(density, a0.at[4:12], local_sem.at[0]),
        pltpu.make_async_copy(material, mat, local_sem.at[1]),
    ]
    for copy in local:
        copy.start()

    barrier = pltpu.get_barrier_semaphore()

    @pl.loop(1, n)
    def _(i):
        pl.semaphore_signal(
            barrier, inc=1, device_id={"depth": lax.rem(d + i, n), "rows": r}, device_id_type=MESH
        )

    for dd in (d_down, d, d_up):
        for rr in (r_down, r_up):
            pl.semaphore_signal(barrier, inc=1, device_id={"depth": dd, "rows": rr}, device_id_type=MESH)
    pl.semaphore_wait(barrier, n - 1 + 6)

    parts = [
        (density.at[4:8], a0.at[0:4], d_up, r),
        (density.at[0:4], a0.at[12:16], d_down, r),
        (density.at[:, 0:4, :], b0.at[4:12, 0:4, :], d, r_down),
        (density.at[:, 4:8, :], b0.at[4:12, 4:8, :], d, r_up),
    ]
    for dd, source, target, step in ((d_up, 7, 3, -1), (d_down, 0, 12, 1)):
        for away in range(3):
            width = 3 - away
            low, high = slice(0, width), slice(SUB - width, SUB)
            parts.append((density.at[source + step * away, low, :], b0.at[target + step * away, low, :], dd, r_down))
            parts.append((density.at[source + step * away, high, :], b0.at[target + step * away, high, :], dd, r_up))
    halo = []
    for index, (source, target, dd, rr) in enumerate(parts):
        copy = pltpu.make_async_remote_copy(
            src_ref=source, dst_ref=target, send_sem=halo_send.at[index], recv_sem=halo_recv.at[index],
            device_id={"depth": dd, "rows": rr}, device_id_type=MESH,
        )
        copy.start()
        halo.append(copy)

    sub = lax.broadcasted_iota(jnp.int32, (SUB, LANES), 0)
    lane = lax.broadcasted_iota(jnp.int32, (SUB, LANES), 1)
    zero = jnp.zeros((SUB, LANES), jnp.float32)

    tables[...] = jnp.zeros_like(tables)
    entries = emission.shape[1]
    for band in range(bands):
        tables[band, :, 0:entries] = jnp.broadcast_to(emission[band : band + 1, :], (SUB, entries))
    tables[bands, :, 0:entries] = jnp.broadcast_to(absorption[...], (SUB, entries))

    for copy in local:
        copy.wait()
    for copy in halo:
        copy.wait()

    @pl.when(d == 0)
    def _():
        a0[0:4] = jnp.zeros((4, SUB, x_size), jnp.float32)
        b0[0:4] = jnp.zeros((4, SUB, x_size), jnp.float32)

    @pl.when(d == n - 1)
    def _():
        a0[12:16] = jnp.zeros((4, SUB, x_size), jnp.float32)
        b0[12:16] = jnp.zeros((4, SUB, x_size), jnp.float32)

    @pl.when(r == 0)
    def _():
        b0[:, 4:8, :] = jnp.zeros((16, 4, x_size), jnp.float32)

    @pl.when(r == n_rows - 1)
    def _():
        b0[:, 0:4, :] = jnp.zeros((16, 4, x_size), jnp.float32)

    coef_low = jnp.where(d > 0, time_step, 0.0)
    coef_high = jnp.where(d < n - 1, time_step, 0.0)
    keep_high_rows = jnp.where(r < n_rows - 1, 1.0, 0.0)
    keep_low_rows = jnp.where(r > 0, 1.0, 0.0)
    keep_b = jnp.where(sub < 4, keep_high_rows, keep_low_rows)

    def span(j):
        return slice(j * LANES, (j + 1) * LANES)

    def row_flux(values):
        fluxes = []
        for j in range(tiles):
            following = values[j + 1] if j + 1 < tiles else zero
            shifted = roll(jnp.where(lane == 0, following, values[j]), LANES - 1, 1)
            fluxes.append(conduct(shifted - values[j]))
        edge = conduct(values[0])
        change = []
        for j in range(tiles):
            before = roll(jnp.where(lane == LANES - 1, fluxes[j - 1], fluxes[j]), 1, 1) if j > 0 else jnp.where(
                lane == 0, edge, roll(fluxes[0], 1, 1)
            )
            change.append(fluxes[j] - before)
        return change

    def layer(z, src_a, src_b, dst_a, dst_b, with_b):
        coef = jnp.where(z < 4, coef_low, jnp.where(z >= 12, coef_high, time_step))
        va = [src_a[z, :, span(j)] for j in range(tiles)]
        vb = [src_b[z, :, span(j)] for j in range(tiles)]
        change = row_flux(va)
        change_b = row_flux(vb) if with_b else None
        for j in range(tiles):
            up_a = roll(jnp.where(sub == 0, vb[j], va[j]), SUB - 1, 0)
            y_a = conduct(up_a - va[j])
            z_a = conduct(src_a[z + 1, :, span(j)] - va[j])
            total_a = change[j] + (z_a - flux_a[:, span(j)])
            flux_a[:, span(j)] = z_a
            if with_b:
                up_b = roll(jnp.where(sub == 0, va[j], vb[j]), SUB - 1, 0)
                y_b = conduct(up_b - vb[j])
                z_b = conduct(src_b[z + 1, :, span(j)] - vb[j])
                total_b = change_b[j] + (z_b - flux_b[:, span(j)])
                flux_b[:, span(j)] = z_b
                total_a = total_a + (y_a - roll(jnp.where(sub == SUB - 1, y_b, y_a), 1, 0))
                total_b = total_b + (y_b - roll(jnp.where(sub == SUB - 1, y_a, y_b), 1, 0))
                dst_b[z, :, span(j)] = vb[j] + (coef * keep_b) * total_b
            else:
                down_a = roll(jnp.where(sub == SUB - 1, vb[j], va[j]), 1, 0)
                total_a = total_a + (y_a + conduct(down_a - va[j]))
            dst_a[z, :, span(j)] = va[j] + coef * total_a

    fields = ((a0, b0), (a1, b1))
    for sweep in range(SWEEPS):
        (src_a, src_b), (dst_a, dst_b) = fields[sweep % 2], fields[(sweep + 1) % 2]
        first, last = 1 + sweep, 14 - sweep
        for j in range(tiles):
            flux_a[:, span(j)] = conduct(src_a[first, :, span(j)] - src_a[first - 1, :, span(j)])
        if sweep + 1 < SWEEPS:
            for j in range(tiles):
                flux_b[:, span(j)] = conduct(src_b[first + 1, :, span(j)] - src_b[first, :, span(j)])
            layer(first, src_a, src_b, dst_a, dst_b, False)

            @pl.loop(first + 1, last)
            def _(z):
                layer(z, src_a, src_b, dst_a, dst_b, True)

            layer(last, src_a, src_b, dst_a, dst_b, False)
        else:

            @pl.loop(first, last + 1)
            def _(z):
                layer(z, src_a, src_b, dst_a, dst_b, False)

    result = pltpu.make_async_copy(a0.at[4:12], smoothed_out, local_sem.at[0])
    result.start()
    for z in range(slab):
        pack_y[0, z : z + 1, :] = a0[4 + z, 0:1, :]
        pack_y[1, z : z + 1, :] = a0[4 + z, SUB - 1 : SUB, :]
    faces = []
    for index, (source, target, dd, rr) in enumerate(
        (
            (a0.at[11], face_z.at[0], d_up, r),
            (a0.at[4], face_z.at[1], d_down, r),
            (pack_y.at[1], face_y.at[0], d, r_up),
            (pack_y.at[0], face_y.at[1], d, r_down),
        )
    ):
        copy = pltpu.make_async_remote_copy(
            src_ref=source, dst_ref=target, send_sem=face_send.at[index], recv_sem=face_recv.at[index],
            device_id={"depth": dd, "rows": rr}, device_id_type=MESH,
        )
        copy.start()
        faces.append(copy)

    step_len = step_scale / (slab * n)

    def lanes(j):
        return pl.ds(pl.multiple_of(j * LANES, LANES), LANES)

    @pl.loop(0, tiles)
    def _(j):
        at = lanes(j)
        depth = zero
        through = jnp.ones((SUB, LANES), jnp.float32)
        for k in range(slab):
            value = a0[4 + k, :, at]
            soft = jnp.maximum(value, 0.0) + jnp.log1p(jnp.exp(-jnp.abs(value)))
            depth = depth + gather(tables[bands], mat[k, :, at]) * soft * step_len
            after = jnp.exp(-depth)
            weight[k, :, at] = through - after
            through = after
        for t in (1, 2, 4):
            sub_bit = lax.rem(lax.div(sub, t), 2)
            lane_bit = lax.rem(lax.div(lane, own * t), 2)
            high = roll(roll(depth, t, 0), LANES - own * t, 1)
            low = roll(roll(depth, SUB - t, 0), own * t, 1)
            depth = jnp.where(sub_bit == lane_bit, depth, jnp.where(sub_bit == 1, high, low))
        depth_send[pl.ds(pl.multiple_of(j * group, group), group), 0, :] = depth

    def send(buffer, target_buffer, which, target):
        return pltpu.make_async_remote_copy(
            src_ref=buffer.at[target], dst_ref=target_buffer.at[d],
            send_sem=a2a_send.at[which], recv_sem=a2a_recv.at[which],
            device_id={"depth": target, "rows": r}, device_id_type=MESH,
        )

    @pl.loop(1, n)
    def _(i):
        send(depth_send, depth_recv, 0, lax.rem(d + i, n)).start()

    depth_recv[d] = depth_send[d]
    for copy in faces:
        copy.wait()

    @pl.when(d == 0)
    def _():
        face_z[0] = jnp.zeros((SUB, x_size), jnp.float32)

    @pl.when(d == n - 1)
    def _():
        face_z[1] = jnp.zeros((SUB, x_size), jnp.float32)

    @pl.when(r == 0)
    def _():
        face_y[0] = jnp.zeros((SUB, x_size), jnp.float32)

    @pl.when(r == n_rows - 1)
    def _():
        face_y[1] = jnp.zeros((SUB, x_size), jnp.float32)

    my_tile = lax.div(d, group)

    @pl.loop(0, tiles)
    def _(i):
        j = lax.rem(my_tile + i, tiles)
        at = lanes(j)
        at_left = lanes(jnp.maximum(j - 1, 0))
        at_right = lanes(jnp.minimum(j + 1, tiles - 1))
        has_left = jnp.where(j > 0, 1.0, 0.0)
        has_right = jnp.where(j < tiles - 1, 1.0, 0.0)
        colour = [zero] * bands
        for k in range(slab):
            value = a0[4 + k, :, at]
            right = roll(jnp.where(lane == 0, a0[4 + k, :, at_right] * has_right, value), LANES - 1, 1)
            left = roll(jnp.where(lane == LANES - 1, a0[4 + k, :, at_left] * has_left, value), 1, 1)
            above = roll(jnp.where(sub == 0, face_y[1, k : k + 1, at], value), SUB - 1, 0)
            below = roll(jnp.where(sub == SUB - 1, face_y[0, k : k + 1, at], value), 1, 0)
            deeper = a0[5 + k, :, at] if k + 1 < slab else face_z[1, :, at]
            nearer = a0[3 + k, :, at] if k > 0 else face_z[0, :, at]
            grad_z = (deeper - nearer) * 0.5
            grad_y = (above - below) * 0.5
            grad_x = (right - left) * 0.5
            lambert = (grad_z * light_z + grad_y * light_y + grad_x * light_x) * lax.rsqrt(
                grad_z * grad_z + grad_y * grad_y + grad_x * grad_x + 1.0
            )
            contrib = weight[k, :, at] * (0.55 + 0.45 * lambert)
            ids = mat[k, :, at]
            for band in range(bands):
                colour[band] = colour[band] + contrib * gather(tables[band], ids)
        for band in range(bands):
            swap[pl.ds(band, SUB, stride=bands), :] = colour[band]
        planes = [swap[y * bands : (y + 1) * bands, :] for y in range(SUB)]
        for t in (1, 2, 4):
            lane_bit = lax.rem(lax.div(lane, own * t), 2) == 0
            updated = list(planes)
            for y in range(SUB):
                if y & t:
                    continue
                low, high = planes[y], planes[y | t]
                updated[y] = jnp.where(lane_bit, low, roll(high, own * t, 1))
                updated[y | t] = jnp.where(lane_bit, roll(low, LANES - own * t, 1), high)
            planes = updated
        for o in range(group):
            colour_send[j * group + o] = planes[o]
        for o in range(group):
            target = j * group + lax.rem(d + o, group)

            @pl.when(target != d)
            def _():
                send(colour_send, colour_recv, 1, target).start()

    colour_recv[d] = colour_send[d]

    def all_of(ref, which):
        return pltpu.make_async_remote_copy(
            src_ref=ref.at[pl.ds(0, n - 1)], dst_ref=ref.at[pl.ds(0, n - 1)],
            send_sem=a2a_send.at[which], recv_sem=a2a_recv.at[which],
            device_id={"depth": d_up, "rows": r}, device_id_type=MESH,
        )

    all_of(depth_recv, 0).wait_recv()
    row_rank = jnp.broadcast_to(rank[...].astype(jnp.float32), (n, n))
    diagonal = lax.broadcasted_iota(jnp.int32, (n, n), 0) == lax.broadcasted_iota(jnp.int32, (n, n), 1)
    column_rank = jnp.sum(jnp.where(diagonal, row_rank, 0.0), axis=1, keepdims=True)
    ahead = jnp.where(row_rank < column_rank, 1.0, 0.0)
    depths = depth_recv[:, 0, :]
    prior = jnp.dot(ahead, depths, precision=lax.Precision.HIGHEST, preferred_element_type=jnp.float32)
    slab_weight[...] = jnp.exp(-prior)
    trans_out[...] = jnp.exp(-jnp.sum(depths, axis=0, keepdims=True))

    all_of(colour_recv, 1).wait_recv()
    total = [zero] * 4
    for s in range(n):
        total[s % 4] = total[s % 4] + slab_weight[s : s + 1, :] * colour_recv[s]
    band_out[...] = (total[0] + total[1]) + (total[2] + total[3])

    all_of(depth_send, 0).wait_send()
    all_of(colour_send, 1).wait_send()
    result.wait()


def solution(mesh):
    n, n_rows = mesh.shape["depth"], mesh.shape["rows"]

    def body(density, material, absorption, emission, shard_rank):
        slab, row_count, x_size = density.shape
        bands, classes = emission.shape
        own = x_size // n
        vmem = pl.BlockSpec(memory_space=pltpu.VMEM)
        hbm = pl.BlockSpec(memory_space=pl.ANY)
        f32 = functools.partial(pltpu.VMEM, dtype=jnp.float32)
        dma = pltpu.SemaphoreType.DMA
        smoothed, band, trans = pl.pallas_call(
            functools.partial(kernel, n, n_rows, x_size),
            out_shape=(
                jax.ShapeDtypeStruct(density.shape, jnp.float32),
                jax.ShapeDtypeStruct((bands, LANES), jnp.float32),
                jax.ShapeDtypeStruct((1, LANES), jnp.float32),
            ),
            in_specs=[hbm, hbm, vmem, vmem, vmem],
            out_specs=(hbm, vmem, vmem),
            scratch_shapes=[
                f32((16, SUB, x_size)), f32((16, SUB, x_size)), f32((16, SUB, x_size)), f32((16, SUB, x_size)),
                f32((SUB, x_size)), f32((SUB, x_size)),
                pltpu.VMEM(material.shape, jnp.int32),
                f32((2, SUB, x_size)), f32((2, SUB, x_size)), f32((2, SUB, x_size)),
                f32(density.shape),
                f32((bands + 1, SUB, LANES)),
                f32((SUB * bands, LANES)),
                f32((n, bands, LANES)), f32((n, 1, LANES)), f32((n, bands, LANES)), f32((n, 1, LANES)),
                f32((n, LANES)),
                dma((2,)), dma((16,)), dma((16,)), dma((4,)), dma((4,)), dma((2,)), dma((2,)),
            ],
            compiler_params=pltpu.CompilerParams(collective_id=0, has_side_effects=True),
        )(density, material, absorption.reshape(1, classes), emission, shard_rank.reshape(1, n))
        return (
            smoothed,
            band.reshape(bands, row_count, own),
            trans.reshape(row_count, own),
        )

    in_specs = (P("depth", "rows", None), P("depth", "rows", None), P(), P(), P())
    out_specs = (P("depth", "rows", None), P(None, "rows", "depth"), P("rows", "depth"))
    return jax.shard_map(body, mesh=mesh, in_specs=in_specs, out_specs=out_specs, check_vma=False)
```

time: 382 us -> 53.7 us (0.14); the launches traced: 377 us -> 53.4 us
  waiting for transfers between devices: 275 us -> 0 us
  starting transfers between devices: 57.5 us -> 0 us
  Pallas kernels: 0 us -> 48.5 us
  between operations: 14.6 us -> 0.66 us
  local copies, waits for them, and re-layouts: 16.8 us -> 3.6 us
  other arithmetic: 10.3 us -> 0.66 us
    unnamed x3 -> x0, waiting for transfers between devices: 148 us -> none
    all_gather x1 -> x0, waiting for transfers between devices: 94.2 us -> none  [body(): block_rows = lax.all_gather(slab_depth[None], 'depth', axis=0, tiled=True)]
    ppermute x20 -> x0, starting transfers between devices: 57.4 us -> none  [the longest x10 33.5 us: with_halo(): lax.ppermute(lax.slice_in_dim(block, block.shape[dim] - width, None, axis...]
    pallas_call x0 -> x1, Pallas kernels: none -> 48.5 us  [body(): pl.pallas_call(functools.partial(kernel, n, n_rows, x_size), out_shape=(j...]
    ppermute x20 -> x0, waiting for transfers between devices: 32.4 us -> none  [the longest x10 32.3 us: with_halo(): lax.ppermute(lax.slice_in_dim(block, 0, width, axis=dim), axis, backward)]
    unnamed x18 -> x5, local copies, waits for them, and re-layouts: 9.63 us -> 1.73 us
    eq x8 -> x0, local copies, waits for them, and re-layouts: 6.11 us -> none  [march(): layer_material[None, :, :] == class_ids[:, None, None]]
  transfers between devices with their start and end apart: 22 -> 0, of which waited for: 11 -> 0; matrix products, arithmetic and copies ran while one was open for 1% -> 0% of each run, Pallas kernels for 0% -> 0%
where the time goes in v1:
time: 53.7 us; the launch traced here: 53.4 us
  Pallas kernels  48.5 us (90%)
  local copies, waits for them, and re-layouts  3.6 us (7%)
  other arithmetic  0.66 us (1%)
  between operations  0.66 us (1%)
    pallas_call x1, Pallas kernels, body(): pl.pallas_call(functools.partial(kernel, n, n_rows, x_size), out_shape=(j...  48.5 us
    unnamed x5, local copies, waits for them, and re-layouts  1.73 us

profile of v1, /device:TPU:1, one launch (start us, length us, event | category | flops | bytes accessed | tf_op | source)
XLA Modules:
  0.0 53.4 jit_solution(12596146912466504722)
XLA Ops:
  0.6 48.5 %shard_map.76 = (f32[8,8,1024]{2,1,0:T(8,128)}, f32[8,128]{1,0:T(8,128)}, f32[1,128]{1,0:T(1,128)}) custom-call(f32[8,8,1024]{2,1,0:T(8,128)} %density.1, s32[8,8,1024]{2,1,0:T(8,128)} %material.1, f32[1,16]{1,0:T(1,128)} %bitcast.2, f32[8,16]{1,0:T(8,128)} %emission.1, s32[1,64]{1,0:T(1,128)} %bitcast.3), custom_call_target="tpu_custom_call" | custom-call | tf_op jit(solution)/shard_map/pallas_call | solution.py:367
  49.2 0.0 copy-start.1
  49.2 0.5 broadcast.3
  49.7 0.0 copy-done.1
  49.7 0.7 %reduce.3 = f32[128]{0:T(128)S(1)} reduce(f32[1,128]{1,0:T(1,128)S(1)} %copy-done.1, f32[]{:T(128)} %broadcast.3), dimensions={0}, to_apply=%get-tuple-element.8.reduce_sub_computation.3 | reduce | bytes 1028 | tf_op jit(solution)/shard_map/pallas_call | solution.py:367
  50.4 0.0 copy-start
  50.4 0.7 %reshape.21 = f32[8,16]{1,0:T(8,128)} reshape(f32[128]{0:T(128)S(1)} %reduce.3) | data formatting | bytes 1024 | tf_op jit(solution)/shard_map/reshape | solution.py:393
  51.1 0.0 copy-done
  51.1 0.7 %reshape.20 = f32[8,8,16]{2,1,0:T(8,128)} reshape(f32[8,128]{1,0:T(8,128)S(1)} %copy-done) | data formatting | bytes 8192 | tf_op jit(solution)/shard_map/reshape | solution.py:392
  51.8 1.7 %copy.9 = f32[8,8,1024]{2,1,0:T(8,128)} copy(f32[8,8,1024]{2,1,0:T(8,128)} %get-tuple-element.12) | data formatting | bytes 524288
Async XLA Ops:
  49.2 0.6 %copy-start.1 = (f32[1,128]{1,0:T(1,128)S(1)}, f32[1,128]{1,0:T(1,128)}, u32[]{:S(2)}) copy-start(f32[1,128]{1,0:T(1,128)} %get-tuple-element.8) | copy-start | bytes 1540
  50.4 0.7 %copy-start = (f32[8,128]{1,0:T(8,128)S(1)}, f32[8,128]{1,0:T(8,128)}, u32[]{:S(2)}) copy-start(f32[8,128]{1,0:T(8,128)} %get-tuple-element.7) | copy-start | bytes 12292

commit v2 on v1

v2 whole, which is shorter than its diff:
```python
import functools

import jax
import jax.numpy as jnp
from jax import lax
from jax.experimental import pallas as pl
from jax.experimental.pallas import tpu as pltpu
from jax.sharding import PartitionSpec as P

MESH = pl.DeviceIdType.MESH
SWEEPS = 4
LANES = 128
SUB = 8
UNROLL = 2
CHIPS_X, CHIPS_Y = 4, 8

time_step = 0.16
edge_scale = 1.5
light_z = 0.6
light_y = 0.48
light_x = 0.64
step_scale = 1.2


def flux(diff):
    return diff / (edge_scale * edge_scale + diff * diff)


def roll(value, shift, axis):
    return pltpu.roll(value, shift % value.shape[axis], axis)


def gather(table, index):
    return jnp.take_along_axis(table, index, axis=1, mode="promise_in_bounds")


def kernel(
    n, n_rows, x_size,
    density, material, absorption, emission, rank,
    smooth, band_out, trans_out,
    a0, a1, b0, b1, flux_a, flux_b, mat, face_z, face_y, pack_y, weight, tables, swap,
    outbox, inbox, slab_weight,
    local_sem, halo_send, halo_recv, face_send, face_recv, a2a_send, a2a_recv, token,
):
    slab, bands = SUB, emission.shape[0]
    tiles = x_size // LANES
    own = x_size // n
    group = LANES // own
    d = lax.axis_index("depth")
    r = lax.axis_index("rows")
    has_depth = {-1: d > 0, 0: None, 1: d < n - 1}
    has_rows = {-1: r > 0, 0: None, 1: r < n_rows - 1}

    def exists(dd, rr):
        conditions = [c for c in (has_depth[dd], has_rows[rr]) if c is not None]
        return functools.reduce(jnp.logical_and, conditions)

    def to(dd, rr):
        return {"depth": d + dd, "rows": r + rr}

    def signal(sem, device):
        pl.semaphore_signal(sem, inc=1, device_id=device, device_id_type=MESH)

    core = lax.rem(d, 2)
    chip_y = lax.rem(lax.div(d, 2), CHIPS_Y)
    chip_x = lax.div(d, 2 * CHIPS_Y)

    def chip(dx, dy, other):
        x = lax.rem(chip_x + (dx + CHIPS_X), CHIPS_X)
        y = lax.rem(chip_y + (dy + CHIPS_Y), CHIPS_Y)
        return {"depth": (x * CHIPS_Y + y) * 2 + (1 - core if other else core), "rows": r}

    barrier = pltpu.get_barrier_semaphore()
    for dd in (-1, 0, 1):
        for rr in (-1, 1):
            pl.when(exists(dd, rr))(functools.partial(signal, barrier, to(dd, rr)))
    close = [
        (dx, dy, other) for dx in (-1, 0, 1) for dy in (-1, 0, 1) for other in (0, 1) if (dx, dy, other) != (0, 0, 0)
    ]
    for offset in close:
        signal(barrier, chip(*offset))

    local = [
        pltpu.make_async_copy(density, a0.at[4:12], local_sem.at[0]),
        pltpu.make_async_copy(material, mat, local_sem.at[1]),
    ]
    for copy in local:
        copy.start()

    def count(conditions):
        return sum(jnp.where(c, 1, 0) for c in conditions)

    beside = count((has_rows[-1], has_rows[1])) * (1 + count((has_depth[-1], has_depth[1])))
    pl.semaphore_wait(barrier, len(close) + beside)

    stages = [[(dx, dy, 0) for dx in (-1, 1) for dy in (-1, 1)], [(0, -2, 0), (0, 2, 0)]]

    def spread(stage):
        if stage > 0:
            for index in range(len(stages[stage - 1])):
                pl.semaphore_wait(token.at[stage - 1, index], 1)
        if stage < len(stages):
            for index, offset in enumerate(stages[stage]):
                signal(token.at[stage, index], chip(*offset))

    def exchange(parts, send_sem, recv_sem):
        copies = []
        for index, (source, target, dd, rr) in enumerate(parts):
            copy = pltpu.make_async_remote_copy(
                src_ref=source, dst_ref=target, send_sem=send_sem.at[index], recv_sem=recv_sem.at[index],
                device_id=to(dd, rr), device_id_type=MESH,
            )
            pl.when(exists(dd, rr))(copy.start)
            copies.append((copy, exists(dd, rr), exists(-dd, -rr)))
        return copies

    def finish(copies):
        for copy, _, arrives in copies:
            pl.when(arrives)(copy.wait_recv)

    def drain(copies):
        for copy, leaves, _ in copies:
            pl.when(leaves)(copy.wait_send)

    parts = [
        (density.at[:, 0:4, :], b0.at[4:12, 0:4, :], 0, -1),
        (density.at[:, 4:8, :], b0.at[4:12, 4:8, :], 0, 1),
        (density.at[4:8], a0.at[0:4], 1, 0),
        (density.at[0:4], a0.at[12:16], -1, 0),
    ]
    for dd, source, target, step in ((1, 7, 3, -1), (-1, 0, 12, 1)):
        for away in range(3):
            width = 3 - away
            low, high = slice(0, width), slice(SUB - width, SUB)
            parts.append((density.at[source + step * away, low, :], b0.at[target + step * away, low, :], dd, -1))
            parts.append((density.at[source + step * away, high, :], b0.at[target + step * away, high, :], dd, 1))
    halo = exchange(parts, halo_send, halo_recv)
    spread(0)

    sub = lax.broadcasted_iota(jnp.int32, (SUB, LANES), 0)
    lane = lax.broadcasted_iota(jnp.int32, (SUB, LANES), 1)
    zero = jnp.zeros((SUB, LANES), jnp.float32)

    tables[...] = jnp.zeros_like(tables)
    entries = emission.shape[1]
    for band in range(bands):
        tables[band, :, 0:entries] = jnp.broadcast_to(emission[band : band + 1, :], (SUB, entries))
    tables[bands, :, 0:entries] = jnp.broadcast_to(absorption[...], (SUB, entries))

    for copy in local:
        copy.wait()
    finish(halo)
    spread(1)

    @pl.when(d == 0)
    def _():
        a0[0:4] = jnp.zeros((4, SUB, x_size), jnp.float32)
        b0[0:4] = jnp.zeros((4, SUB, x_size), jnp.float32)

    @pl.when(d == n - 1)
    def _():
        a0[12:16] = jnp.zeros((4, SUB, x_size), jnp.float32)
        b0[12:16] = jnp.zeros((4, SUB, x_size), jnp.float32)

    @pl.when(r == 0)
    def _():
        b0[:, 4:8, :] = jnp.zeros((16, 4, x_size), jnp.float32)

    @pl.when(r == n_rows - 1)
    def _():
        b0[:, 0:4, :] = jnp.zeros((16, 4, x_size), jnp.float32)

    scale = time_step * edge_scale * edge_scale
    coef_low = jnp.where(d > 0, scale, 0.0)
    coef_high = jnp.where(d < n - 1, scale, 0.0)
    keep_high_rows = jnp.where(r < n_rows - 1, 1.0, 0.0)
    keep_low_rows = jnp.where(r > 0, 1.0, 0.0)
    keep_b = jnp.where(sub < 4, keep_high_rows, keep_low_rows)

    def span(j):
        return slice(j * LANES, (j + 1) * LANES)

    def along_row(value, following, before):
        shifted = roll(jnp.where(lane == 0, following, value), LANES - 1, 1)
        out = flux(shifted - value)
        if before is None:
            back = jnp.where(lane == 0, flux(value), roll(out, 1, 1))
        else:
            back = roll(jnp.where(lane == LANES - 1, before, out), 1, 1)
        return out, out - back

    def layer(z, src_a, src_b, dst_a, dst_b, with_b, offset=0):
        coef = jnp.where(z < 4, coef_low, jnp.where(z >= 12, coef_high, scale))
        x_a = x_b = None
        for j in range(tiles):
            here, beyond = span(j), span(j + 1)
            a, b = src_a[z, :, here], src_b[z, :, here]
            x_a, total_a = along_row(a, src_a[z, :, beyond] if j + 1 < tiles else zero, x_a)
            z_a = flux(src_a[z + 1, :, here] - a)
            total_a = total_a + (z_a - flux_a[:, here])
            flux_a[:, here] = z_a
            y_a = flux(roll(jnp.where(sub == 0, b, a), SUB - 1, 0) - a)
            if with_b:
                x_b, total_b = along_row(b, src_b[z, :, beyond] if j + 1 < tiles else zero, x_b)
                z_b = flux(src_b[z + 1, :, here] - b)
                total_b = total_b + (z_b - flux_b[:, here])
                flux_b[:, here] = z_b
                y_b = flux(roll(jnp.where(sub == 0, a, b), SUB - 1, 0) - b)
                total_a = total_a + (y_a - roll(jnp.where(sub == SUB - 1, y_b, y_a), 1, 0))
                total_b = total_b + (y_b - roll(jnp.where(sub == SUB - 1, y_a, y_b), 1, 0))
                dst_b[z, :, here] = b + (coef * keep_b) * total_b
            else:
                total_a = total_a + (y_a + flux(roll(jnp.where(sub == SUB - 1, b, a), 1, 0) - a))
            dst_a[z - offset, :, here] = a + coef * total_a

    fields = ((a0, b0), (a1, b1))
    for sweep in range(SWEEPS):
        (src_a, src_b), (dst_a, dst_b) = fields[sweep % 2], fields[(sweep + 1) % 2]
        first, last = 1 + sweep, 14 - sweep
        for j in range(tiles):
            flux_a[:, span(j)] = flux(src_a[first, :, span(j)] - src_a[first - 1, :, span(j)])
        if sweep + 1 < SWEEPS:
            for j in range(tiles):
                flux_b[:, span(j)] = flux(src_b[first + 1, :, span(j)] - src_b[first, :, span(j)])
            layer(first, src_a, src_b, dst_a, dst_b, False)

            @pl.loop(0, last - first - 1, unroll=UNROLL)
            def _(i):
                layer(first + 1 + i, src_a, src_b, dst_a, dst_b, True)

            layer(last, src_a, src_b, dst_a, dst_b, False)
        else:

            @pl.loop(0, last + 1 - first, unroll=UNROLL)
            def _(i):
                layer(first + i, src_a, src_b, smooth, None, False, 4)

    for z in range(slab):
        pack_y[0, z : z + 1, :] = smooth[z, 0:1, :]
        pack_y[1, z : z + 1, :] = smooth[z, SUB - 1 : SUB, :]
    faces = exchange(
        (
            (pack_y.at[1], face_y.at[0], 0, 1),
            (pack_y.at[0], face_y.at[1], 0, -1),
            (smooth.at[slab - 1], face_z.at[0], 1, 0),
            (smooth.at[0], face_z.at[1], -1, 0),
        ),
        face_send, face_recv,
    )

    step_len = step_scale / (slab * n)

    def lanes(j):
        return pl.ds(pl.multiple_of(j * LANES, LANES), LANES)

    @pl.loop(0, tiles)
    def _(j):
        at = lanes(j)
        depth = zero
        through = jnp.ones((SUB, LANES), jnp.float32)
        for k in range(slab):
            value = smooth[k, :, at]
            soft = jnp.maximum(value, 0.0) + jnp.log1p(jnp.exp(-jnp.abs(value)))
            depth = depth + gather(tables[bands], mat[k, :, at]) * soft * step_len
            after = jnp.exp(-depth)
            weight[k, :, at] = through - after
            through = after
        for t in (1, 2, 4):
            sub_bit = lax.rem(lax.div(sub, t), 2)
            lane_bit = lax.rem(lax.div(lane, own * t), 2)
            high = roll(roll(depth, t, 0), LANES - own * t, 1)
            low = roll(roll(depth, SUB - t, 0), own * t, 1)
            depth = jnp.where(sub_bit == lane_bit, depth, jnp.where(sub_bit == 1, high, low))
        outbox[pl.ds(pl.multiple_of(j * group, group), group), bands, :] = depth

    spread(2)
    finish(faces)

    @pl.when(d == 0)
    def _():
        face_z[0] = jnp.zeros((SUB, x_size), jnp.float32)

    @pl.when(d == n - 1)
    def _():
        face_z[1] = jnp.zeros((SUB, x_size), jnp.float32)

    @pl.when(r == 0)
    def _():
        face_y[0] = jnp.zeros((SUB, x_size), jnp.float32)

    @pl.when(r == n_rows - 1)
    def _():
        face_y[1] = jnp.zeros((SUB, x_size), jnp.float32)

    my_tile = lax.div(d, group)

    def tile_of(i):
        return lax.rem(my_tile + 1 + i, tiles)

    def post(i, first):
        for o in range(first, group):
            target = tile_of(i) * group + lax.rem(d + o, group)
            pltpu.make_async_remote_copy(
                src_ref=outbox.at[target], dst_ref=inbox.at[d], send_sem=a2a_send, recv_sem=a2a_recv,
                device_id={"depth": target, "rows": r}, device_id_type=MESH,
            ).start()

    def shade(i):
        j = tile_of(i)
        at = lanes(j)
        at_left = lanes(jnp.maximum(j - 1, 0))
        at_right = lanes(jnp.minimum(j + 1, tiles - 1))
        has_left = jnp.where(j > 0, 1.0, 0.0)
        has_right = jnp.where(j < tiles - 1, 1.0, 0.0)
        colour = [zero] * bands
        for k in range(slab):
            value = smooth[k, :, at]
            right = roll(jnp.where(lane == 0, smooth[k, :, at_right] * has_right, value), LANES - 1, 1)
            left = roll(jnp.where(lane == LANES - 1, smooth[k, :, at_left] * has_left, value), 1, 1)
            above = roll(jnp.where(sub == 0, face_y[1, k : k + 1, at], value), SUB - 1, 0)
            below = roll(jnp.where(sub == SUB - 1, face_y[0, k : k + 1, at], value), 1, 0)
            deeper = smooth[k + 1, :, at] if k + 1 < slab else face_z[1, :, at]
            nearer = smooth[k - 1, :, at] if k > 0 else face_z[0, :, at]
            grad_z = (deeper - nearer) * 0.5
            grad_y = (above - below) * 0.5
            grad_x = (right - left) * 0.5
            lambert = (grad_z * light_z + grad_y * light_y + grad_x * light_x) * lax.rsqrt(
                grad_z * grad_z + grad_y * grad_y + grad_x * grad_x + 1.0
            )
            contrib = weight[k, :, at] * (0.55 + 0.45 * lambert)
            ids = mat[k, :, at]
            for band in range(bands):
                colour[band] = colour[band] + contrib * gather(tables[band], ids)
        for band in range(bands):
            swap[pl.ds(band, SUB, stride=bands), :] = colour[band]
        planes = [swap[y * bands : (y + 1) * bands, :] for y in range(SUB)]
        for t in (1, 2, 4):
            lane_bit = lax.rem(lax.div(lane, own * t), 2) == 0
            updated = list(planes)
            for y in range(SUB):
                if y & t:
                    continue
                low, high = planes[y], planes[y | t]
                updated[y] = jnp.where(lane_bit, low, roll(high, own * t, 1))
                updated[y | t] = jnp.where(lane_bit, roll(low, LANES - own * t, 1), high)
            planes = updated
        for o in range(group):
            outbox[j * group + o, 0:bands, :] = planes[o]

    shade(0)

    @pl.loop(1, tiles)
    def _(i):
        post(i - 1, 0)
        shade(i)

    post(tiles - 1, 1)
    inbox[d] = outbox[d]

    def all_of(ref):
        return pltpu.make_async_remote_copy(
            src_ref=ref.at[pl.ds(0, n - 1)], dst_ref=ref.at[pl.ds(0, n - 1)], send_sem=a2a_send, recv_sem=a2a_recv,
            device_id=chip(0, 0, 1), device_id_type=MESH,
        )

    all_of(inbox).wait_recv()
    row_rank = jnp.broadcast_to(rank[...].astype(jnp.float32), (n, n))
    diagonal = lax.broadcasted_iota(jnp.int32, (n, n), 0) == lax.broadcasted_iota(jnp.int32, (n, n), 1)
    column_rank = jnp.sum(jnp.where(diagonal, row_rank, 0.0), axis=1, keepdims=True)
    ahead = jnp.where(row_rank < column_rank, 1.0, 0.0)
    depths = inbox[:, bands, :]
    prior = jnp.dot(ahead, depths, precision=lax.Precision.HIGHEST, preferred_element_type=jnp.float32)
    slab_weight[...] = jnp.exp(-prior)
    trans_out[...] = jnp.exp(-jnp.sum(depths, axis=0, keepdims=True))

    total = [zero] * 4
    for s in range(n):
        total[s % 4] = total[s % 4] + slab_weight[s : s + 1, :] * inbox[s, 0:bands, :]
    band_out[...] = (total[0] + total[1]) + (total[2] + total[3])

    drain(halo)
    drain(faces)
    all_of(outbox).wait_send()


def place(own, smooth, band, trans, smoothed_out, band_out, trans_out, sem):
    outward = pltpu.make_async_copy(smooth, smoothed_out, sem)
    outward.start()
    for y in range(SUB):
        lanes = slice(y * own, (y + 1) * own)
        for b in range(band.shape[0]):
            band_out[b, y : y + 1, :] = band[b : b + 1, lanes]
        trans_out[y : y + 1, :] = trans[:, lanes]
    outward.wait()


def solution(mesh):
    n, n_rows = mesh.shape["depth"], mesh.shape["rows"]

    def body(density, material, absorption, emission, shard_rank):
        slab, row_count, x_size = density.shape
        bands, classes = emission.shape
        own = x_size // n
        vmem = pl.BlockSpec(memory_space=pltpu.VMEM)
        hbm = pl.BlockSpec(memory_space=pl.ANY)
        f32 = functools.partial(pltpu.VMEM, dtype=jnp.float32)
        dma = pltpu.SemaphoreType.DMA
        smoothed, band, trans = pl.pallas_call(
            functools.partial(kernel, n, n_rows, x_size),
            out_shape=(f32(density.shape), f32((bands, LANES)), f32((1, LANES))),
            in_specs=[hbm, hbm, vmem, vmem, vmem],
            out_specs=(vmem, vmem, vmem),
            scratch_shapes=[
                f32((16, SUB, x_size)), f32((16, SUB, x_size)), f32((16, SUB, x_size)), f32((16, SUB, x_size)),
                f32((SUB, x_size)), f32((SUB, x_size)),
                pltpu.VMEM(material.shape, jnp.int32),
                f32((2, SUB, x_size)), f32((2, SUB, x_size)), f32((2, SUB, x_size)),
                f32(density.shape),
                f32((bands + 1, SUB, LANES)),
                f32((SUB * bands, LANES)),
                f32((n, bands + 1, LANES)), f32((n, bands + 1, LANES)),
                f32((n, LANES)),
                dma((2,)), dma((16,)), dma((16,)), dma((4,)), dma((4,)), dma, dma, pltpu.SemaphoreType.REGULAR((2, 4)),
            ],
            compiler_params=pltpu.CompilerParams(collective_id=0, has_side_effects=True),
        )(density, material, absorption.reshape(1, classes), emission, shard_rank.reshape(1, n))
        return pl.pallas_call(
            functools.partial(place, own),
            out_shape=(
                jax.ShapeDtypeStruct(density.shape, jnp.float32),
                jax.ShapeDtypeStruct((bands, row_count, own), jnp.float32),
                jax.ShapeDtypeStruct((row_count, own), jnp.float32),
            ),
            in_specs=[vmem, vmem, vmem],
            out_specs=(hbm, vmem, vmem),
            scratch_shapes=[dma],
        )(*(pltpu.with_memory_space_constraint(x, pltpu.VMEM) for x in (smoothed, band, trans)))

    in_specs = (P("depth", "rows", None), P("depth", "rows", None), P(), P(), P())
    out_specs = (P("depth", "rows", None), P(None, "rows", "depth"), P("rows", "depth"))
    return jax.shard_map(body, mesh=mesh, in_specs=in_specs, out_specs=out_specs, check_vma=False)
```

time: 53.7 us -> 37.5 us (0.70)
  Pallas kernels: 48.5 us -> 36.3 us
  local copies, waits for them, and re-layouts: 3.6 us -> 0 us
  other arithmetic: 0.66 us -> 0 us
    pallas_call x1 -> x2, Pallas kernels: 48.5 us -> 36.3 us  [the longest x1 34.9 us: body(): pl.pallas_call(functools.partial(kernel, n, n_rows, x_size), out_shape=(f...]
    unnamed x5 -> x0, local copies, waits for them, and re-layouts: 1.73 us -> none
    reshape x2 -> x0, local copies, waits for them, and re-layouts: 1.36 us -> none  [the longest x1 0.69 us: body(): band.reshape(bands, row_count, own)]
    pallas_call x1 -> x0, other arithmetic: 0.66 us -> none  [body(): pl.pallas_call(functools.partial(kernel, n, n_rows, x_size), out_shape=(j...]
where the time goes in v2:
time: 37.5 us; the launch traced here: 36.9 us
  Pallas kernels  36.3 us (97%)
  between operations  0.64 us (2%)
    pallas_call x1, Pallas kernels, body(): pl.pallas_call(functools.partial(kernel, n, n_rows, x_size), out_shape=(f...  34.9 us
    pallas_call x1, Pallas kernels, body(): pl.pallas_call(functools.partial(place, own), out_shape=(jax.ShapeDtypeSt...  1.33 us

profile of v2, /device:TPU:1, one launch (start us, length us, event | category | flops | bytes accessed | tf_op | source)
XLA Modules:
  0.0 36.9 jit_solution(15070433950481050280)
XLA Ops:
  0.6 34.9 %shard_map.76 = (f32[8,8,1024]{2,1,0:T(8,128)S(1)}, f32[8,128]{1,0:T(8,128)S(1)}, f32[1,128]{1,0:T(1,128)S(1)}) custom-call(f32[8,8,1024]{2,1,0:T(8,128)} %density.1, s32[8,8,1024]{2,1,0:T(8,128)} %material.1, f32[1,16]{1,0:T(1,128)} %bitcast.2, f32[8,16]{1,0:T(8,128)} %emission.1, s32[1,64]{1,0:T(1,128)} %bitcast.3), custom_call_target="tpu_custom_call" | custom-call | tf_op jit(solution)/shard_map/pallas_call | solution.py:408
  35.6 1.3 %shard_map.77 = (f32[8,8,1024]{2,1,0:T(8,128)}, f32[8,8,16]{2,1,0:T(8,128)}, f32[8,16]{1,0:T(8,128)}) custom-call(f32[8,8,1024]{2,1,0:T(8,128)S(1)} %get-tuple-element.6.smooth, f32[8,128]{1,0:T(8,128)S(1)} %get-tuple-element.7.band, f32[1,128]{1,0:T(1,128)S(1)} %get-tuple-element.8.trans), custom_call_target="tpu_custom_call" | custom-call | tf_op jit(solution)/shard_map/pallas_call | solution.py:427

commit v3 on v2

--- a/solution.py
+++ b/solution.py
@@ -36,10 +36,10 @@
 
 def kernel(
     n, n_rows, x_size,
-    density, material, absorption, emission, rank,
+    density, material, absorption_in, emission_in, rank_in,
     smooth, band_out, trans_out,
     a0, a1, b0, b1, flux_a, flux_b, mat, face_z, face_y, pack_y, weight, tables, swap,
-    outbox, inbox, slab_weight,
+    outbox, inbox, slab_weight, absorption, emission, rank, ahead,
     local_sem, halo_send, halo_recv, face_send, face_recv, a2a_send, a2a_recv, token,
 ):
     slab, bands = SUB, emission.shape[0]
@@ -82,7 +82,10 @@
 
     local = [
         pltpu.make_async_copy(density, a0.at[4:12], local_sem.at[0]),
-        pltpu.make_async_copy(material, mat, local_sem.at[1]),
+        pltpu.make_async_copy(emission_in, emission, local_sem.at[1]),
+        pltpu.make_async_copy(absorption_in, absorption, local_sem.at[2]),
+        pltpu.make_async_copy(rank_in, rank, local_sem.at[3]),
+        pltpu.make_async_copy(material, mat, local_sem.at[4]),
     ]
     for copy in local:
         copy.start()
@@ -103,11 +106,11 @@
             for index, offset in enumerate(stages[stage]):
                 signal(token.at[stage, index], chip(*offset))
 
-    def exchange(parts, send_sem, recv_sem):
+    def exchange(parts, send_sem, recv_sem, base=0):
         copies = []
         for index, (source, target, dd, rr) in enumerate(parts):
             copy = pltpu.make_async_remote_copy(
-                src_ref=source, dst_ref=target, send_sem=send_sem.at[index], recv_sem=recv_sem.at[index],
+                src_ref=source, dst_ref=target, send_sem=send_sem.at[base + index], recv_sem=recv_sem.at[base + index],
                 device_id=to(dd, rr), device_id_type=MESH,
             )
             pl.when(exists(dd, rr))(copy.start)
@@ -135,23 +138,21 @@
             parts.append((density.at[source + step * away, low, :], b0.at[target + step * away, low, :], dd, -1))
             parts.append((density.at[source + step * away, high, :], b0.at[target + step * away, high, :], dd, 1))
     halo = exchange(parts, halo_send, halo_recv)
+    beside_halo, corner_halo = halo[:4], halo[4:]
     spread(0)
 
     sub = lax.broadcasted_iota(jnp.int32, (SUB, LANES), 0)
     lane = lax.broadcasted_iota(jnp.int32, (SUB, LANES), 1)
     zero = jnp.zeros((SUB, LANES), jnp.float32)
 
+    for copy in local:
+        copy.wait()
     tables[...] = jnp.zeros_like(tables)
     entries = emission.shape[1]
     for band in range(bands):
         tables[band, :, 0:entries] = jnp.broadcast_to(emission[band : band + 1, :], (SUB, entries))
     tables[bands, :, 0:entries] = jnp.broadcast_to(absorption[...], (SUB, entries))
 
-    for copy in local:
-        copy.wait()
-    finish(halo)
-    spread(1)
-
     @pl.when(d == 0)
     def _():
         a0[0:4] = jnp.zeros((4, SUB, x_size), jnp.float32)
@@ -169,6 +170,29 @@
     @pl.when(r == n_rows - 1)
     def _():
         b0[:, 0:4, :] = jnp.zeros((16, 4, x_size), jnp.float32)
+
+    @pl.when(d == 0)
+    def _():
+        face_z[0] = jnp.zeros((SUB, x_size), jnp.float32)
+
+    @pl.when(d == n - 1)
+    def _():
+        face_z[1] = jnp.zeros((SUB, x_size), jnp.float32)
+
+    @pl.when(r == 0)
+    def _():
+        face_y[0] = jnp.zeros((SUB, x_size), jnp.float32)
+
+    @pl.when(r == n_rows - 1)
+    def _():
+        face_y[1] = jnp.zeros((SUB, x_size), jnp.float32)
+
+    row_rank = jnp.broadcast_to(rank[...].astype(jnp.float32), (n, n))
+    diagonal = lax.broadcasted_iota(jnp.int32, (n, n), 0) == lax.broadcasted_iota(jnp.int32, (n, n), 1)
+    column_rank = jnp.sum(jnp.where(diagonal, row_rank, 0.0), axis=1, keepdims=True)
+    ahead[...] = jnp.where(row_rank < column_rank, 1.0, 0.0)
+    spread(1)
+    finish(beside_halo)
 
     scale = time_step * edge_scale * edge_scale
     coef_low = jnp.where(d > 0, scale, 0.0)
@@ -217,35 +241,67 @@
     for sweep in range(SWEEPS):
         (src_a, src_b), (dst_a, dst_b) = fields[sweep % 2], fields[(sweep + 1) % 2]
         first, last = 1 + sweep, 14 - sweep
-        for j in range(tiles):
-            flux_a[:, span(j)] = flux(src_a[first, :, span(j)] - src_a[first - 1, :, span(j)])
-        if sweep + 1 < SWEEPS:
+
+        def start(z, with_a=True, with_b=True):
             for j in range(tiles):
-                flux_b[:, span(j)] = flux(src_b[first + 1, :, span(j)] - src_b[first, :, span(j)])
-            layer(first, src_a, src_b, dst_a, dst_b, False)
+                if with_a:
+                    flux_a[:, span(j)] = flux(src_a[z, :, span(j)] - src_a[z - 1, :, span(j)])
+                if with_b:
+                    flux_b[:, span(j)] = flux(src_b[z, :, span(j)] - src_b[z - 1, :, span(j)])
+
+        def both(z):
+            layer(z, src_a, src_b, dst_a, dst_b, True)
+
+        def only_a(z):
+            layer(z, src_a, src_b, dst_a, dst_b, False)
+
+        if sweep == 0:
+            start(5)
+
+            @pl.loop(0, slab - 2, unroll=UNROLL)
+            def _(i):
+                both(5 + i)
+
+            finish(corner_halo)
+            for z in (11, 12, 13):
+                both(z)
+            only_a(14)
+            start(1, with_b=False)
+            start(2, with_a=False)
+            for z in (1, 2, 3, 4):
+                (only_a if z == 1 else both)(z)
+            drain(halo)
+        elif sweep + 1 < SWEEPS:
+            start(first, with_b=False)
+            start(first + 1, with_a=False)
+            only_a(first)
 
             @pl.loop(0, last - first - 1, unroll=UNROLL)
             def _(i):
-                layer(first + 1 + i, src_a, src_b, dst_a, dst_b, True)
-
-            layer(last, src_a, src_b, dst_a, dst_b, False)
+                both(first + 1 + i)
+
+            only_a(last)
         else:
-
-            @pl.loop(0, last + 1 - first, unroll=UNROLL)
+            def final(z):
+                layer(z, src_a, src_b, smooth, None, False, 4)
+
+            start(last, with_b=False)
+            final(last)
+            start(first, with_b=False)
+            final(first)
+            deep_faces = exchange(
+                ((smooth.at[slab - 1], face_z.at[0], 1, 0), (smooth.at[0], face_z.at[1], -1, 0)), face_send, face_recv
+            )
+
+            @pl.loop(1, last - first, unroll=UNROLL)
             def _(i):
-                layer(first + i, src_a, src_b, smooth, None, False, 4)
+                final(first + i)
 
     for z in range(slab):
         pack_y[0, z : z + 1, :] = smooth[z, 0:1, :]
         pack_y[1, z : z + 1, :] = smooth[z, SUB - 1 : SUB, :]
-    faces = exchange(
-        (
-            (pack_y.at[1], face_y.at[0], 0, 1),
-            (pack_y.at[0], face_y.at[1], 0, -1),
-            (smooth.at[slab - 1], face_z.at[0], 1, 0),
-            (smooth.at[0], face_z.at[1], -1, 0),
-        ),
-        face_send, face_recv,
+    faces = deep_faces + exchange(
+        ((pack_y.at[1], face_y.at[0], 0, 1), (pack_y.at[0], face_y.at[1], 0, -1)), face_send, face_recv, 2
     )
 
     step_len = step_scale / (slab * n)
@@ -253,7 +309,7 @@
     def lanes(j):
         return pl.ds(pl.multiple_of(j * LANES, LANES), LANES)
 
-    @pl.loop(0, tiles)
+    @pl.loop(0, tiles, unroll=UNROLL)
     def _(j):
         at = lanes(j)
         depth = zero
@@ -273,37 +329,22 @@
             depth = jnp.where(sub_bit == lane_bit, depth, jnp.where(sub_bit == 1, high, low))
         outbox[pl.ds(pl.multiple_of(j * group, group), group), bands, :] = depth
 
-    spread(2)
     finish(faces)
 
-    @pl.when(d == 0)
-    def _():
-        face_z[0] = jnp.zeros((SUB, x_size), jnp.float32)
-
-    @pl.when(d == n - 1)
-    def _():
-        face_z[1] = jnp.zeros((SUB, x_size), jnp.float32)
-
-    @pl.when(r == 0)
-    def _():
-        face_y[0] = jnp.zeros((SUB, x_size), jnp.float32)
-
-    @pl.when(r == n_rows - 1)
-    def _():
-        face_y[1] = jnp.zeros((SUB, x_size), jnp.float32)
-
     my_tile = lax.div(d, group)
 
+    order = [5, 3, 4, 7, 1, 2, 6, 0]
+
     def tile_of(i):
-        return lax.rem(my_tile + 1 + i, tiles)
+        return i
 
     def post(i, first):
         for o in range(first, group):
             target = tile_of(i) * group + lax.rem(d + o, group)
-            pltpu.make_async_remote_copy(
+            pl.when(target != d)(pltpu.make_async_remote_copy(
                 src_ref=outbox.at[target], dst_ref=inbox.at[d], send_sem=a2a_send, recv_sem=a2a_recv,
                 device_id={"depth": target, "rows": r}, device_id_type=MESH,
-            ).start()
+            ).start)
 
     def shade(i):
         j = tile_of(i)
@@ -332,8 +373,8 @@
             for band in range(bands):
                 colour[band] = colour[band] + contrib * gather(tables[band], ids)
         for band in range(bands):
-            swap[pl.ds(band, SUB, stride=bands), :] = colour[band]
-        planes = [swap[y * bands : (y + 1) * bands, :] for y in range(SUB)]
+            swap[i % 2, pl.ds(band, SUB, stride=bands), :] = colour[band]
+        planes = [swap[i % 2, y * bands : (y + 1) * bands, :] for y in range(SUB)]
         for t in (1, 2, 4):
             lane_bit = lax.rem(lax.div(lane, own * t), 2) == 0
             updated = list(planes)
@@ -347,14 +388,15 @@
         for o in range(group):
             outbox[j * group + o, 0:bands, :] = planes[o]
 
-    shade(0)
-
-    @pl.loop(1, tiles)
-    def _(i):
-        post(i - 1, 0)
+    for i in range(tiles):
+        if i == 2:
+            spread(2)
+        if i % 2 == 0 and i > 0:
+            post(i - 2, 0)
+            post(i - 1, 0)
         shade(i)
-
-    post(tiles - 1, 1)
+    post(tiles - 2, 0)
+    post(tiles - 1, 0)
     inbox[d] = outbox[d]
 
     def all_of(ref):
@@ -364,12 +406,8 @@
         )
 
     all_of(inbox).wait_recv()
-    row_rank = jnp.broadcast_to(rank[...].astype(jnp.float32), (n, n))
-    diagonal = lax.broadcasted_iota(jnp.int32, (n, n), 0) == lax.broadcasted_iota(jnp.int32, (n, n), 1)
-    column_rank = jnp.sum(jnp.where(diagonal, row_rank, 0.0), axis=1, keepdims=True)
-    ahead = jnp.where(row_rank < column_rank, 1.0, 0.0)
     depths = inbox[:, bands, :]
-    prior = jnp.dot(ahead, depths, precision=lax.Precision.HIGHEST, preferred_element_type=jnp.float32)
+    prior = jnp.dot(ahead[...], depths, precision=lax.Precision.HIGHEST, preferred_element_type=jnp.float32)
     slab_weight[...] = jnp.exp(-prior)
     trans_out[...] = jnp.exp(-jnp.sum(depths, axis=0, keepdims=True))
 
@@ -378,7 +416,6 @@
         total[s % 4] = total[s % 4] + slab_weight[s : s + 1, :] * inbox[s, 0:bands, :]
     band_out[...] = (total[0] + total[1]) + (total[2] + total[3])
 
-    drain(halo)
     drain(faces)
     all_of(outbox).wait_send()
 
@@ -408,7 +445,7 @@
         smoothed, band, trans = pl.pallas_call(
             functools.partial(kernel, n, n_rows, x_size),
             out_shape=(f32(density.shape), f32((bands, LANES)), f32((1, LANES))),
-            in_specs=[hbm, hbm, vmem, vmem, vmem],
+            in_specs=[hbm, hbm, hbm, hbm, hbm],
             out_specs=(vmem, vmem, vmem),
             scratch_shapes=[
                 f32((16, SUB, x_size)), f32((16, SUB, x_size)), f32((16, SUB, x_size)), f32((16, SUB, x_size)),
@@ -417,10 +454,10 @@
                 f32((2, SUB, x_size)), f32((2, SUB, x_size)), f32((2, SUB, x_size)),
                 f32(density.shape),
                 f32((bands + 1, SUB, LANES)),
-                f32((SUB * bands, LANES)),
+                f32((2, SUB * bands, LANES)),
                 f32((n, bands + 1, LANES)), f32((n, bands + 1, LANES)),
-                f32((n, LANES)),
-                dma((2,)), dma((16,)), dma((16,)), dma((4,)), dma((4,)), dma, dma, pltpu.SemaphoreType.REGULAR((2, 4)),
+                f32((n, LANES)), f32((1, classes)), f32((bands, classes)), pltpu.VMEM((1, n), jnp.int32), f32((n, n)),
+                dma((5,)), dma((16,)), dma((16,)), dma((4,)), dma((4,)), dma, dma, pltpu.SemaphoreType.REGULAR((2, 4)),
             ],
             compiler_params=pltpu.CompilerParams(collective_id=0, has_side_effects=True),
         )(density, material, absorption.reshape(1, classes), emission, shard_rank.reshape(1, n))

time: 37.5 us -> 35.7 us (0.952)
  the two profiles are of different devices: /device:TPU:1 before, /device:TPU:31 now
where the time goes in v3:
time: 35.7 us; the launch traced here: 35.6 us
  Pallas kernels  34.9 us (98%)
  between operations  0.64 us (2%)
    pallas_call x1, Pallas kernels, body(): pl.pallas_call(functools.partial(kernel, n, n_rows, x_size), out_shape=(f...  33.6 us
    pallas_call x1, Pallas kernels, body(): pl.pallas_call(functools.partial(place, own), out_shape=(jax.ShapeDtypeSt...  1.33 us

profile of v3, /device:TPU:31, one launch (start us, length us, event | category | flops | bytes accessed | tf_op | source)
XLA Modules:
  0.0 35.6 jit_solution(16676284475539086236)
XLA Ops:
  0.6 33.6 %shard_map.76 = (f32[8,8,1024]{2,1,0:T(8,128)S(1)}, f32[8,128]{1,0:T(8,128)S(1)}, f32[1,128]{1,0:T(1,128)S(1)}) custom-call(f32[8,8,1024]{2,1,0:T(8,128)} %density.1, s32[8,8,1024]{2,1,0:T(8,128)} %material.1, f32[1,16]{1,0:T(1,128)} %bitcast.2, f32[8,16]{1,0:T(8,128)} %emission_in.1, s32[1,64]{1,0:T(1,128)} %bitcast.3), custom_call_target="tpu_custom_call" | custom-call | tf_op jit(solution)/shard_map/pallas_call | solution.py:445
  34.2 1.3 %shard_map.77 = (f32[8,8,1024]{2,1,0:T(8,128)}, f32[8,8,16]{2,1,0:T(8,128)}, f32[8,16]{1,0:T(8,128)}) custom-call(f32[8,8,1024]{2,1,0:T(8,128)S(1)} %get-tuple-element.6.smooth, f32[8,128]{1,0:T(8,128)S(1)} %get-tuple-element.7.band, f32[1,128]{1,0:T(1,128)S(1)} %get-tuple-element.8.trans), custom_call_target="tpu_custom_call" | custom-call | tf_op jit(solution)/shard_map/pallas_call | solution.py:464

commit v4 on v3

--- a/solution.py
+++ b/solution.py
@@ -258,7 +258,7 @@
         if sweep == 0:
             start(5)
 
-            @pl.loop(0, slab - 2, unroll=UNROLL)
+            @pl.loop(0, slab - 2, unroll=3)
             def _(i):
                 both(5 + i)
 
@@ -276,7 +276,7 @@
             start(first + 1, with_a=False)
             only_a(first)
 
-            @pl.loop(0, last - first - 1, unroll=UNROLL)
+            @pl.loop(0, last - first - 1, unroll=5 if (last - first - 1) % 5 == 0 else 4)
             def _(i):
                 both(first + 1 + i)
 
@@ -293,7 +293,7 @@
                 ((smooth.at[slab - 1], face_z.at[0], 1, 0), (smooth.at[0], face_z.at[1], -1, 0)), face_send, face_recv
             )
 
-            @pl.loop(1, last - first, unroll=UNROLL)
+            @pl.loop(1, last - first, unroll=3)
             def _(i):
                 final(first + i)
 
@@ -309,7 +309,7 @@
     def lanes(j):
         return pl.ds(pl.multiple_of(j * LANES, LANES), LANES)
 
-    @pl.loop(0, tiles, unroll=UNROLL)
+    @pl.loop(0, tiles, unroll=4)
     def _(j):
         at = lanes(j)
         depth = zero

time: 35.7 us -> 35.3 us (0.989)
  Pallas kernels: 34.9 us -> 34.5 us
    pallas_call x1, Pallas kernels: 33.6 us -> 33.2 us  [body(): pl.pallas_call(functools.partial(kernel, n, n_rows, x_size), out_shape=(f...]
where the time goes in v4:
time: 35.3 us; the launch traced here: 35.2 us
  Pallas kernels  34.5 us (98%)
  between operations  0.64 us (2%)
    pallas_call x1, Pallas kernels, body(): pl.pallas_call(functools.partial(kernel, n, n_rows, x_size), out_shape=(f...  33.2 us
    pallas_call x1, Pallas kernels, body(): pl.pallas_call(functools.partial(place, own), out_shape=(jax.ShapeDtypeSt...  1.33 us

profile of v4, /device:TPU:31, one launch (start us, length us, event | category | flops | bytes accessed | tf_op | source)
XLA Modules:
  0.0 35.2 jit_solution(11383321657295603312)
XLA Ops:
  0.6 33.2 %shard_map.76 = (f32[8,8,1024]{2,1,0:T(8,128)S(1)}, f32[8,128]{1,0:T(8,128)S(1)}, f32[1,128]{1,0:T(1,128)S(1)}) custom-call(f32[8,8,1024]{2,1,0:T(8,128)} %density.1, s32[8,8,1024]{2,1,0:T(8,128)} %material.1, f32[1,16]{1,0:T(1,128)} %bitcast.2, f32[8,16]{1,0:T(8,128)} %emission_in.1, s32[1,64]{1,0:T(1,128)} %bitcast.3), custom_call_target="tpu_custom_call" | custom-call | tf_op jit(solution)/shard_map/pallas_call | solution.py:445
  33.8 1.3 %shard_map.77 = (f32[8,8,1024]{2,1,0:T(8,128)}, f32[8,8,16]{2,1,0:T(8,128)}, f32[8,16]{1,0:T(8,128)}) custom-call(f32[8,8,1024]{2,1,0:T(8,128)S(1)} %get-tuple-element.6.smooth, f32[8,128]{1,0:T(8,128)S(1)} %get-tuple-element.7.band, f32[1,128]{1,0:T(1,128)S(1)} %get-tuple-element.8.trans), custom_call_target="tpu_custom_call" | custom-call | tf_op jit(solution)/shard_map/pallas_call | solution.py:464
